TPU v7x, 32 devices: a whole 2x2x4 slice. The times are simulated.
32 devices in a mesh: row: 8 (over z, x), col: 4 (over y, core).
Axes of the slice: x: 2, y: 2, z: 4, core: 2. Of those that a mesh axis runs over, the one named last changes fastest.
Arguments:
- trailing: float32 [8192, 1536], P('row', 'col'), may hold values from -6 to 6
- reflectors: float32 [8192, 256], P('row', 'col'), may hold values from -6 to 6
- factor: float32 [256, 256], replicated, as said below
- column_sums: float32 [8192, 8], P('row', 'col'), may hold values from -6 to 6
- row_sums: float32 [16, 1536], P('row', 'col'), may hold values from -6 to 6
Outputs:
- updated: float32 [8192, 1536], P('row', 'col')
- column_checks: float32 [8192, 8], P('row', 'col')
- row_checks: float32 [16, 1536], P('row', 'col')
Inputs may be any that keep to these rules, and one draw needn't show every extreme that they name: `factor`: zero below the diagonal.
All inputs are finite; a program needn't handle non-finite values.
Results may differ from a plain program's by a relative error of at most 0.000067.
Values sent between devices are 32-bit elements; how exact they have to be, the bound alone decides.
No kernel may reach another device: no remote copies, remote signals or barrier semaphores. Data moves between devices by JAX's collectives and lax.ppermute only.
A program may use at most 64 MiB of HBM per device.

v0:
```python
import jax
import jax.numpy as jnp
from jax import lax
from jax.sharding import PartitionSpec as P


def matmul(left, right):
    return jnp.dot(left, right, precision=lax.Precision.HIGHEST, preferred_element_type=jnp.float32)


def shards(trailing, reflectors, factor, column_sums, row_sums):
    panel = lax.all_gather(reflectors, "col", axis=1, tiled=True)
    columns = trailing.shape[1]
    joined = jnp.concatenate([trailing, column_sums], axis=1)
    product = matmul(panel.T, joined)
    product_main = product[:, :columns]
    product_check = product[:, columns:]
    summed_main, summed_check = lax.psum((product_main, product_check), "row")
    main_image = matmul(factor.T, summed_main)
    check_image = matmul(factor.T, summed_check)
    updated = trailing - matmul(panel, main_image)
    column_checks = column_sums - matmul(panel, check_image)
    count = trailing.shape[0]
    local = jnp.arange(count).astype(jnp.float32)
    scale = 1.0 / jnp.sqrt(jnp.float32(count))
    weights = jnp.stack([jnp.ones((count,), jnp.float32) * scale, (local + 1.0) * scale / count])
    check_coeff = matmul(weights, panel)
    row_checks = row_sums - matmul(check_coeff, main_image)
    return (updated, column_checks, row_checks)


def solution(mesh):
    placed = (P("row", "col"), P("row", "col"), P(), P("row", "col"), P("row", "col"))
    return jax.shard_map(
        shards,
        mesh=mesh,
        in_specs=placed,
        out_specs=(P("row", "col"), P("row", "col"), P("row", "col")),
        check_vma=False,
    )
```

profile of v0, /device:TPU:0, one launch (start us, length us, event | category | flops | bytes accessed | tf_op | source)
XLA Modules:
  0.0 139.2 jit_solution(17977182560160107712)
XLA Ops:
  7.2 0.0 copy-start
  7.2 0.0 all-gather.2.cloned.1.call-start
  7.2 0.7 all-gather.2.cloned.1.call-update
  7.9 0.0 all-reduce.3.cloned.1.call-start
  8.0 0.9 copy.8
  8.9 0.0 copy-start.2
  8.9 3.1 %copy.9 = f32[1024,384]{0,1:T(8,128)} copy(f32[1024,384]{1,0:T(8,128)} %param.5) | data formatting | bytes 3145728 | tf_op args[0]
  12.0 17.0 %all-gather.2.cloned.1.call-done = f32[1024,256]{0,1:T(8,128)} async-done(((f32[1024,64]{0,1:T(8,128)}), f32[1024,256]{0,1:T(8,128)}) %all-gather.2.cloned.1.call-update) | async-done | bytes 1048592 | tf_op jit(solution)/shard_map/all_gather | solution.py:12
  29.0 0.0 copy-done.2
  29.0 0.0 copy-start.1
  29.0 4.7 %fusion.4 = f32[256,386]{0,1:T(8,128)S(1)} fusion(f32[1024,256]{0,1:T(8,128)} %all-gather.2.cloned.1.call-done, f32[1024,2]{1,0:T(8,128)S(1)} %copy.8, f32[1024,384]{1,0:T(8,128)S(1)} %copy-done.2), kind=kOutput, calls=%fused_computation.5 | convolution fusion | flops 1214646272 | bytes 3024896 | tf_op jit(solution)/shard_map/dot_general | solution.py:8
  33.8 0.0 copy-start.4
  33.8 0.8 slice.8
  34.5 21.3 %psum.15 = f32[256,2]{0,1:T(2,128)S(1)} all-reduce(f32[256,2]{0,1:T(2,128)S(1)} %slice.9), channel_id=1, replica_groups=mesh['row'=8,'col'=4] {'row'}, use_global_device_ids=true, to_apply=%region_1.0 | all-reduce | flops 512 | bytes 4096 | tf_op jit(solution)/shard_map/psum | solution.py:18
  55.9 0.0 all-reduce.3.cloned.1.call-update
  55.9 0.0 copy-done.1
  55.9 0.0 copy-start.3
  55.9 0.9 fusion.8
  56.8 0.0 copy-done
  56.8 0.2 fusion.13
  57.0 0.0 copy-done.4
  57.1 1.2 fusion.7
  58.3 65.9 %all-reduce.3.cloned.1.call-done = f32[256,384]{0,1:T(8,128)} async-done(((f32[256,384]{0,1:T(8,128)}), f32[256,384]{0,1:T(8,128)}) %all-reduce.3.cloned.1.call-update) | async-done | bytes 393232 | tf_op jit(solution)/shard_map/psum | solution.py:18
  124.2 1.5 %fusion.12 = f32[384,256]{1,0:T(8,128)S(1)} fusion(f32[256,384]{0,1:T(8,128)} %all-reduce.3.cloned.1.call-done, f32[256,256]{1,0:T(8,128)S(1)} %copy-done), kind=kOutput, calls=%fused_computation.14 | convolution fusion | flops 301989888 | bytes 1048576 | tf_op jit(solution)/shard_map/dot_general | solution.py:8
  125.7 0.0 copy-done.3
  125.7 2.6 %bitcast_subtract_fusion = f32[1024,384]{0,1:T(8,128)} fusion(f32[1024,384]{0,1:T(8,128)S(1)} %copy-done.3, f32[384,256]{1,0:T(8,128)S(1)} %fusion.12, f32[1024,256]{0,1:T(8,128)S(1)} %copy-done.1), kind=kOutput, calls=%fused_computation.4 | convolution fusion | flops 1208352768 | bytes 4587520 | tf_op jit(solution)/shard_map/dot_general | solution.py:8
  128.3 0.0 copy-start.5
  128.3 3.0 %copy.10 = f32[1024,384]{1,0:T(8,128)} copy(f32[1024,384]{0,1:T(8,128)} %bitcast_subtract_fusion) | data formatting | bytes 3145728
  131.4 0.0 copy-done.5
  131.4 1.0 convolution_subtract_fusion
  (2 shorter events, 0.0 us)
Async XLA Ops:
  7.2 49.7 %copy-start = (f32[256,256]{1,0:T(8,128)S(1)}, f32[256,256]{1,0:T(8,128)}, u32[]{:S(2)}) copy-start(f32[256,256]{1,0:T(8,128)} %param.7) | copy-start | bytes 786436
  7.2 21.8 %all-gather.2.cloned.1.call-start = ((), (), s32[]{:S(2)}) async-start(), calls=%async_computation | async-start | bytes 1310720 | tf_op jit(solution)/shard_map/all_gather | solution.py:12
  7.9 116.3 %all-reduce.3.cloned.1.call-start = ((), (), s32[]{:S(2)}) async-start(), calls=%async_computation.1 | async-start | bytes 786432 | tf_op jit(solution)/shard_map/psum | solution.py:18
  8.9 20.1 %copy-start.2 = (f32[1024,384]{1,0:T(8,128)S(1)}, f32[1024,384]{1,0:T(8,128)}, u32[]{:S(2)}) copy-start(f32[1024,384]{1,0:T(8,128)} %param.5) | copy-start | bytes 4718596
  29.0 26.9 %copy-start.1 = (f32[1024,256]{0,1:T(8,128)S(1)}, f32[1024,256]{0,1:T(8,128)}, u32[]{:S(2)}) copy-start(f32[1024,256]{0,1:T(8,128)} %all-gather.2.cloned.1.call-done) | copy-start | bytes 3145732
  33.8 23.3 %copy-start.4 = (f32[1024,2]{0,1:T(2,128)S(1)}, f32[1024,2]{0,1:T(2,128)}, u32[]{:S(2)}) copy-start(f32[1024,2]{0,1:T(2,128)} %param.8) | copy-start | bytes 24580
  55.9 69.8 %copy-start.3 = (f32[1024,384]{0,1:T(8,128)S(1)}, f32[1024,384]{0,1:T(8,128)}, u32[]{:S(2)}) copy-start(f32[1024,384]{0,1:T(8,128)} %copy.9) | copy-start | bytes 4718596
  128.3 3.0 %copy-start.5 = (f32[2,384]{1,0:T(2,128)S(1)}, f32[2,384]{1,0:T(2,128)}, u32[]{:S(2)}) copy-start(f32[2,384]{1,0:T(2,128)} %param.9) | copy-start | bytes 9220
Sparse Core Ops, SparseCore 0:
  9.5 19.4 all-gather.1
  56.0 68.1 all-reduce.2
where the time goes:
time: 139 us
  waiting for transfers between devices  83.6 us (60%)
  blocking collectives  21.3 us (15%)
  between operations  14.1 us (10%)
  matrix products  12.2 us (9%)
  local copies, waits for them, and re-layouts  7.89 us (6%)
    psum x1, waiting for transfers between devices, shards(): summed_main, summed_check = lax.psum((product_main, product_check), 'row')  65.9 us
    psum x1, blocking collectives, shards(): summed_main, summed_check = lax.psum((product_main, product_check), 'row')  21.3 us
    all_gather x1, waiting for transfers between devices, shards(): panel = lax.all_gather(reflectors, 'col', axis=1, tiled=True)  17 us
    dot_general x7, matrix products, matmul(): jnp.dot(left, right, precision=lax.Precision.HIGHEST, preferred_element_t...  12.2 us
    unnamed x15, local copies, waits for them, and re-layouts  7.12 us
  transfers between devices with their start and end apart: 2, of which 2 were waited for; matrix products, arithmetic and copies ran while one was open for 5% of the time, Pallas kernels for 0%

commit v1 on v0

--- a/solution.py
+++ b/solution.py
@@ -9,7 +9,26 @@
 
 
 def shards(trailing, reflectors, factor, column_sums, row_sums):
-    panel = lax.all_gather(reflectors, "col", axis=1, tiled=True)
+    size, index, rows = (lax.axis_size("col"), lax.axis_index("col"), reflectors.shape[1])
+    right_2 = [(i, (i + 1) % size) for i in range(size)]
+    behind = [(i, (i - 1) % size) for i in range(size)]
+    whole = jnp.zeros(
+        (*reflectors.shape[:1], size * rows, *reflectors.shape[1 + 1 :]), reflectors.dtype
+    )
+    whole = lax.dynamic_update_slice_in_dim(whole, reflectors, index * rows, axis=1)
+    from_left = from_right = reflectors
+    half = size // 2
+    for step in range(1, half + 1):
+        from_left = lax.ppermute(from_left, "col", right_2)
+        whole = lax.dynamic_update_slice_in_dim(
+            whole, from_left, (index - step) % size * rows, axis=1
+        )
+        if step < size - half:
+            from_right = lax.ppermute(from_right, "col", behind)
+            whole = lax.dynamic_update_slice_in_dim(
+                whole, from_right, (index + step) % size * rows, axis=1
+            )
+    panel = whole
     columns = trailing.shape[1]
     joined = jnp.concatenate([trailing, column_sums], axis=1)
     product = matmul(panel.T, joined)

time: 139 us -> 117 us (0.84)
  waiting for transfers between devices: 83.6 us -> 54.8 us
  starting transfers between devices: 0.08 us -> 5.03 us
  blocking collectives: 21.3 us -> 23.3 us
    all_gather x1 -> x0, waiting for transfers between devices: 17 us -> none  [shards(): panel = lax.all_gather(reflectors, 'col', axis=1, tiled=True)]
    psum x1, waiting for transfers between devices: 65.9 us -> 50.1 us  [shards(): summed_main, summed_check = lax.psum((product_main, product_check), 'row')]
    unnamed x15 -> x11, local copies, waits for them, and re-layouts: 7.12 us -> 0.99 us
    ppermute x0 -> x3, starting transfers between devices: none -> 4.99 us  [the longest x2 2.98 us: shards(): from_left = lax.ppermute(from_left, 'col', right_2)]
    ppermute x0 -> x3, waiting for transfers between devices: none -> 4.69 us  [the longest x2 4.68 us: shards(): from_left = lax.ppermute(from_left, 'col', right_2)]
    dynamic_update_slice x0 -> x4, local copies, waits for them, and re-layouts: none -> 4.01 us  [the longest x2 1.94 us: shards(): lax.dynamic_update_slice_in_dim(whole, from_left, (index - step) % size *...]
    psum x1, blocking collectives: 21.3 us -> 23.3 us  [shards(): summed_main, summed_check = lax.psum((product_main, product_check), 'row')]
  transfers between devices with their start and end apart: 2 -> 4, of which waited for: 2 -> 3; matrix products, arithmetic and copies ran while one was open for 5% -> 5% of each run, Pallas kernels for 0% -> 0%
where the time goes in v1:
time: 117 us
  waiting for transfers between devices  54.8 us (47%)
  blocking collectives  23.3 us (20%)
  between operations  14.2 us (12%)
  matrix products  12.9 us (11%)
  local copies, waits for them, and re-layouts  6.58 us (6%)
  starting transfers between devices  5.03 us (4%)
    psum x1, waiting for transfers between devices, shards(): summed_main, summed_check = lax.psum((product_main, product_check), 'row')  50.1 us
    psum x1, blocking collectives, shards(): summed_main, summed_check = lax.psum((product_main, product_check), 'row')  23.3 us
    dot_general x7, matrix products, matmul(): jnp.dot(left, right, precision=lax.Precision.HIGHEST, preferred_element_t...  12.9 us
    ppermute x2, waiting for transfers between devices, shards(): from_left = lax.ppermute(from_left, 'col', right_2)  4.68 us
    ppermute x2, starting transfers between devices, shards(): from_left = lax.ppermute(from_left, 'col', right_2)  2.98 us
  transfers between devices with their start and end apart: 4, of which 3 were waited for; matrix products, arithmetic and copies ran while one was open for 5% of the time, Pallas kernels for 0%

profile of v1, /device:TPU:0, one launch (start us, length us, event | category | flops | bytes accessed | tf_op | source)
XLA Modules:
  0.0 116.9 jit_solution(137318740897264365)
XLA Ops:
  7.2 0.0 copy-start
  7.2 0.0 copy-start.3
  7.2 0.0 all-reduce.3.cloned.1.call-start
  7.2 0.5 collective-permute-start
  7.8 2.0 %collective-permute-start.1 = (f32[1024,64]{0,1:T(8,128)}, f32[1024,64]{0,1:T(8,128)}, u32[]{:S(2)}, u32[]{:S(2)}) collective-permute-start(f32[1024,64]{0,1:T(8,128)} %param.6), channel_id=1, source_target_pairs={{0,3},{1,0},{2,1},{3,2},{4,7},{5,4},{6,5},{7,6},{8,11},{9,8},{10,9... | collective-permute-start | bytes 786440 | tf_op jit(solution)/shard_map/ppermute | solution.py:27
  9.8 0.1 broadcast_in_dim.3
  9.9 0.0 copy-start.1
  9.9 1.1 constant_dynamic-update-slice_fusion.3
  11.0 3.3 %collective-permute-done = f32[1024,64]{0,1:T(8,128)} collective-permute-done((f32[1024,64]{0,1:T(8,128)}, f32[1024,64]{0,1:T(8,128)}, u32[]{:S(2)}, u32[]{:S(2)}) %collective-permute-start) | collective-permute-done | bytes 262176 | tf_op jit(solution)/shard_map/ppermute | solution.py:22
  14.3 2.4 %collective-permute-start.2 = (f32[1024,64]{0,1:T(8,128)}, f32[1024,64]{0,1:T(8,128)}, u32[]{:S(2)}, u32[]{:S(2)}) collective-permute-start(f32[1024,64]{0,1:T(8,128)} %collective-permute-done), channel_id=1, source_target_pairs={{0,1},{1,2},{2,3},{3,0},{4,5},{5,6},{6,7},{7,4},{8,9},{9,10},{10,1... | collective-permute-start | bytes 786440 | tf_op jit(solution)/shard_map/ppermute | solution.py:22
  16.8 0.0 copy-done.3
  16.8 0.2 copy.8
  17.1 1.0 constant_dynamic-update-slice_fusion.2
  18.0 0.0 collective-permute-done.1
  18.1 1.0 constant_dynamic-update-slice_fusion.1
  19.0 1.4 %collective-permute-done.2 = f32[1024,64]{0,1:T(8,128)} collective-permute-done((f32[1024,64]{0,1:T(8,128)}, f32[1024,64]{0,1:T(8,128)}, u32[]{:S(2)}, u32[]{:S(2)}) %collective-permute-start.2) | collective-permute-done | bytes 262176 | tf_op jit(solution)/shard_map/ppermute | solution.py:22
  20.4 1.0 constant_dynamic-update-slice_fusion
  21.4 0.0 copy-done.1
  21.4 3.4 %fusion = f32[256,386]{0,1:T(8,128)S(1)} fusion(f32[1024,256]{0,1:T(8,128)S(1)} %constant_dynamic-update-slice_fusion, f32[1024,2]{1,0:T(8,128)S(1)} %copy.8, f32[1024,384]{1,0:T(8,128)S(1)} %copy-done.1), kind=kOutput, calls=%fused_computation | convolution fusion | flops 1214646272 | bytes 3024896 | tf_op jit(solution)/shard_map/dot_general | solution.py:8
  24.9 0.0 copy-start.2
  24.9 0.7 copy-done.2
  25.6 0.8 slice.8
  26.4 0.7 slice.9
  27.1 0.0 all-reduce.3.cloned.1.call-update
  27.1 0.9 fusion.4
  28.0 23.3 %psum.15 = f32[256,2]{0,1:T(2,128)S(1)} all-reduce(f32[256,2]{0,1:T(2,128)S(1)} %slice.9), channel_id=1, replica_groups=mesh['row'=8,'col'=4] {'row'}, use_global_device_ids=true, to_apply=%region_1.2 | all-reduce | flops 512 | bytes 4096 | tf_op jit(solution)/shard_map/psum | solution.py:37
  51.3 0.0 copy-done
  51.3 0.2 fusion.9
  51.5 1.3 %convolution_subtract_fusion.1 = f32[1024,2]{0,1:T(2,128)} fusion(f32[1024,2]{0,1:T(2,128)S(1)} %copy-done.3, f32[1024,256]{0,1:T(8,128)S(1)} %constant_dynamic-update-slice_fusion, f32[2,256]{1,0:T(2,128)S(1)} %fusion.9), kind=kOutput, calls=%fused_computation.5 | convolution fusion | flops 6293504 | bytes 1067008 | tf_op jit(solution)/shard_map/dot_general | solution.py:8
  52.8 50.1 %all-reduce.3.cloned.1.call-done = f32[256,384]{0,1:T(8,128)} async-done(((f32[256,384]{0,1:T(8,128)}), f32[256,384]{0,1:T(8,128)}) %all-reduce.3.cloned.1.call-update) | async-done | bytes 393232 | tf_op jit(solution)/shard_map/psum | solution.py:37
  102.9 1.5 %fusion.8 = f32[384,256]{1,0:T(8,128)S(1)} fusion(f32[256,384]{0,1:T(8,128)} %all-reduce.3.cloned.1.call-done, f32[256,256]{1,0:T(8,128)S(1)} %copy-done), kind=kOutput, calls=%fused_computation.16 | convolution fusion | flops 301989888 | bytes 1048576 | tf_op jit(solution)/shard_map/dot_general | solution.py:8
  104.4 0.0 copy-start.4
  104.4 4.6 %convolution_subtract_fusion = f32[1024,384]{1,0:T(8,128)} fusion(f32[1024,384]{1,0:T(8,128)S(1)} %copy-done.1, f32[1024,256]{0,1:T(8,128)S(1)} %constant_dynamic-update-slice_fusion, f32[384,256]{1,0:T(8,128)S(1)} %fusion.8), kind=kOutput, calls=%fused_computation.4 | convolution fusion | flops 1208352768 | bytes 4587520 | tf_op jit(solution)/shard_map/dot_general | solution.py:8
  109.0 0.0 copy-done.4
  109.0 1.0 convolution_subtract_fusion.2
  (1 shorter events, 0.0 us)
Async XLA Ops:
  7.2 44.2 %copy-start = (f32[256,256]{1,0:T(8,128)S(1)}, f32[256,256]{1,0:T(8,128)}, u32[]{:S(2)}) copy-start(f32[256,256]{1,0:T(8,128)} %param.7) | copy-start | bytes 786436
  7.2 9.6 %copy-start.3 = (f32[1024,2]{0,1:T(2,128)S(1)}, f32[1024,2]{0,1:T(2,128)}, u32[]{:S(2)}) copy-start(f32[1024,2]{0,1:T(2,128)} %param.8) | copy-start | bytes 24580
  7.2 95.7 %all-reduce.3.cloned.1.call-start = ((), (), s32[]{:S(2)}) async-start(), calls=%async_computation | async-start | bytes 786432 | tf_op jit(solution)/shard_map/psum | solution.py:37
  7.2 7.1 %collective-permute-start = (f32[1024,64]{0,1:T(8,128)}, f32[1024,64]{0,1:T(8,128)}, u32[]{:S(2)}, u32[]{:S(2)}) collective-permute-start(f32[1024,64]{0,1:T(8,128)} %param.6), channel_id=1, source_target_pairs={{0,1},{1,2},{2,3},{3,0},{4,5},{5,6},{6,7},{7,4},{8,9},{9,10},{10,1... | collective-permute-start | bytes 786440 | tf_op jit(solution)/shard_map/ppermute | solution.py:22
  7.8 10.3 %collective-permute-start.1 = (f32[1024,64]{0,1:T(8,128)}, f32[1024,64]{0,1:T(8,128)}, u32[]{:S(2)}, u32[]{:S(2)}) collective-permute-start(f32[1024,64]{0,1:T(8,128)} %param.6), channel_id=1, source_target_pairs={{0,3},{1,0},{2,1},{3,2},{4,7},{5,4},{6,5},{7,6},{8,11},{9,8},{10,9... | collective-permute-start | bytes 786440 | tf_op jit(solution)/shard_map/ppermute | solution.py:27
  9.9 11.5 %copy-start.1 = (f32[1024,384]{1,0:T(8,128)S(1)}, f32[1024,384]{1,0:T(8,128)}, u32[]{:S(2)}) copy-start(f32[1024,384]{1,0:T(8,128)} %param.5) | copy-start | bytes 4718596
  14.3 6.1 %collective-permute-start.2 = (f32[1024,64]{0,1:T(8,128)}, f32[1024,64]{0,1:T(8,128)}, u32[]{:S(2)}, u32[]{:S(2)}) collective-permute-start(f32[1024,64]{0,1:T(8,128)} %collective-permute-done), channel_id=1, source_target_pairs={{0,1},{1,2},{2,3},{3,0},{4,5},{5,6},{6,7},{7,4},{8,9},{9,10},{10,1... | collective-permute-start | bytes 786440 | tf_op jit(solution)/shard_map/ppermute | solution.py:22
  24.9 0.8 copy-start.2
  104.4 4.6 %copy-start.4 = (f32[2,384]{1,0:T(2,128)S(1)}, f32[2,384]{1,0:T(2,128)}, u32[]{:S(2)}) copy-start(f32[2,384]{1,0:T(2,128)} %param.9) | copy-start | bytes 9220
Sparse Core Ops, SparseCore 0:
  27.2 75.6 all-reduce.2
